TPU v7x, 32 devices: a whole 2x2x4 slice. The times are simulated.
32 devices in a mesh: ckpt: 4 (over x, core), wide: 8 (over z, y).
Axes of the slice: x: 2, y: 2, z: 4, core: 2. Of those that a mesh axis runs over, the one named last changes fastest.
Arguments:
- codes: bfloat16 [4, 8, 8192, 1024], P('ckpt', 'wide'), may hold values from -4 to 4
- scales: float32 [4, 8, 8192, 8], P('ckpt', 'wide'), may hold values from 0.5 to 5
- example_ids: int32 [8, 8192], P('wide'), may hold values from 0 to 8191, each once within a row
- targets: bfloat16 [1024, 4096], P('wide'), may hold values from -0.09375 to 0.09375
- owners: int32 [6], replicated, may hold values from 0 to 7, as said below
Outputs:
- scores: float32 [8, 8192, 768], P('wide', 'ckpt')
Inputs may be any that keep to these rules, and one draw needn't show every extreme that they name: `example_ids`: each row is a permutation of the 8192 examples of its group. Distinct owners; owner 0 and owner 8 - 1 are always among them.
All inputs are finite; a program needn't handle non-finite values.
Results may differ from a plain program's by a relative error of at most 0.0029.
Values may be sent and summed in bfloat16 or wider, within the bound.
A program may use at most 192 MiB of HBM per device.

v0:
```python
import jax
import jax.numpy as jnp
from jax import lax
from jax.sharding import PartitionSpec as P


def from_root(shard, axis, root):
    mine = lax.axis_index(axis) == root
    return lax.psum(jnp.where(mine, shard, jnp.zeros_like(shard)), axis)


def fetch(targets, owner, width):
    piece = lax.dynamic_slice_in_dim(targets, lax.axis_index("ckpt") * width, width, 1)
    got = from_root(piece, "wide", owner)
    return lax.all_gather(got, "ckpt", axis=1, tiled=True)


def per_device(codes, scales, example_ids, targets, owners):
    width = codes.shape[-1]
    block = width // scales.shape[-1]
    feats = (codes[0, 0].astype(jnp.float32) * jnp.repeat(scales[0, 0], block, axis=-1)).astype(
        jnp.bfloat16
    )
    ordered = jnp.take(feats, example_ids[0], axis=0)
    rounds = owners.shape[0]
    contract = (((1,), (1,)), ((), ()))
    resident = lax.all_to_all(ordered, "ckpt", split_axis=0, concat_axis=1, tiled=True)
    columns = []
    for step in range(rounds):
        chosen = fetch(targets, owners[step], width)
        columns.append(
            lax.dot_general(resident, chosen, contract, preferred_element_type=jnp.float32)
        )
    result = jnp.concatenate(columns, axis=1)
    scale_factor = 1.0 / lax.axis_size("ckpt")
    return (result * scale_factor)[None]


def solution(mesh):
    return jax.shard_map(
        per_device,
        mesh=mesh,
        in_specs=(
            P("ckpt", "wide", None, None),
            P("ckpt", "wide", None, None),
            P("wide", None),
            P("wide", None),
            P(),
        ),
        out_specs=P("wide", "ckpt", None),
        check_vma=False,
    )
```

profile of v0, /device:TPU:0, one launch (start us, length us, event | category | flops | bytes accessed | tf_op | source)
XLA Modules:
  0.0 415.8 jit_solution(499906623515090295)
XLA Ops:
  6.5 3.5 copy.8
  10.1 0.8 compare_select_fusion
  10.9 10.3 %broadcast_in_dim.15 = f32[8192,8,128]{2,1,0:T(8,128)S(1)} broadcast(f32[8192,8]{1,0:T(8,128)} %copy.8), dimensions={0,1} | broadcast | bytes 33816576 | tf_op jit(solution)/shard_map/broadcast_in_dim | solution.py:21
  21.2 18.0 %fusion = bf16[8192,1024]{1,0:T(8,128)(2,1)} fusion(f32[1024,8,8,128]{3,2,1,0:T(8,128)S(1)} %bitcast.58, bf16[1,1,8192,1024]{3,2,1,0:T(8,128)(2,1)} %param.5), kind=kLoop, calls=%fused_computation.2 | loop fusion | flops 25165824 | bytes 67108864 | tf_op jit(solution)/shard_map/convert_element_type | solution.py:21
  39.1 48.4 %gather_fusion = bf16[8192,1024]{1,0:T(8,128)(2,1)} fusion(bf16[8192,1024]{1,0:T(8,128)(2,1)} %fusion, s32[8192]{0:T(1024)S(1)} %broadcast_clamp_fusion), kind=kCustom, calls=%fused_computation | custom fusion | bytes 33587200 | tf_op jit(solution)/shard_map/jit(_take)/gather | solution.py:24
  87.6 21.9 %copy.9 = bf16[4,2048,1024]{1,2,0:T(8,128)(2,1)} copy(bf16[4,2048,1024]{2,1,0:T(8,128)(2,1)} %bitcast.59) | data formatting | bytes 33554432 | tf_op jit(solution)/shard_map/jit(_take)/gather | solution.py:24
  109.5 0.5 broadcast.55
  110.0 0.7 reduce.3
  110.8 14.2 %broadcast_select_fusion = bf16[4,2048,1024]{1,2,0:T(8,128)(2,1)} fusion(bf16[4,2048,1024]{1,2,0:T(8,128)(2,1)} %copy.9, pred[4,2048]{1,0:T(4,128)(4,1)S(1)} %compare_and_fusion), kind=kLoop, calls=%fused_computation.3 | loop fusion | flops 8388608 | bytes 33562624 | tf_op jit(solution)/shard_map/jit(_take)/select_n | solution.py:24
  125.0 7.1 %all-to-all-start = ((bf16[4,2048,1024]{1,2,0:T(8,128)(2,1)}), bf16[4,2048,1024]{1,2,0:T(8,128)(2,1)}, u32[]{:S(2)}, u32[]{:S(2)}) async-start(bf16[4,2048,1024]{1,2,0:T(8,128)(2,1)} %broadcast_select_fusion), calls=%async_computation | async-start | bytes 33554432 | tf_op jit(solution)/shard_map/all_to_all | solution.py:27
  132.1 0.0 all-reduce.3.cloned.1.call-start
  132.1 0.7 fusion.7
  136.6 2.2 broadcast_select_fusion.1
  138.8 0.0 all-gather.7.cloned.1.call-start
  138.8 93.2 %all-reduce.3.cloned.1.call-done = (bf16[128,1024]{1,0:T(8,128)(2,1)}, bf16[128,1024]{1,0:T(8,128)(2,1)}, bf16[128,1024]{1,0:T(8,128)(2,1)}, bf16[128,1024]{1,0:...) async-done(((bf16[128,1024]{1,0:T(8,128)(2,1)}, bf16[128,1024]{1,0:T(8,128)(2,1)}, bf16[128,1024]{1,0:T(8,128)(2,1)}, bf16[128,1024]{1,0:T(8,128)(2,1)}, ...) | async-done | bytes 1572880 | tf_op jit(solution)/shard_map/psum | solution.py:9
  232.0 0.0 all-gather.9.cloned.1.call-start
  232.1 0.7 all-gather.9.cloned.1.call-update
  232.8 0.5 all-gather.11.cloned.1.call-update
  233.4 0.5 all-gather.13.cloned.1.call-update
  234.0 0.5 all-gather.15.cloned.1.call-update
  234.5 0.2 all-gather.17.cloned.1.call-start
  234.7 0.5 all-gather.17.cloned.1.call-update
  235.2 19.7 %all-gather.7.cloned.1.call-done = bf16[128,4096]{1,0:T(8,128)(2,1)} async-done(((bf16[128,1024]{1,0:T(8,128)(2,1)}), bf16[128,4096]{1,0:T(8,128)(2,1)}) %all-gather.7.cloned.1.call-update) | async-done | bytes 1048592 | tf_op jit(solution)/shard_map/all_gather | solution.py:15
  255.0 83.9 %all-to-all-done = bf16[4,2048,1024]{1,2,0:T(8,128)(2,1)} async-done(((bf16[4,2048,1024]{1,2,0:T(8,128)(2,1)}), bf16[4,2048,1024]{1,2,0:T(8,128)(2,1)}, u32[]{:S(2)}, u32[]{:S(2)}) %all-to-all-start) | async-done | bytes 16777248 | tf_op jit(solution)/shard_map/all_to_all | solution.py:27
  338.9 9.5 %fusion.6 = f32[1,2048,768]{1,2,0:T(8,128)} fusion(bf16[128,4096]{1,0:T(8,128)(2,1)} %all-gather.7.cloned.1.call-done, bf16[2048,4096]{0,1:T(8,128)(2,1)} %bitcast.6), kind=kOutput, calls=%fused_computation.16 | convolution fusion | flops 2147483648 | bytes 18874368 | tf_op jit(solution)/shard_map/dot_general | solution.py:32
  348.4 9.5 %fusion.5 = f32[1,2048,768]{1,2,0:T(8,128)} fusion(f32[1,2048,768]{1,2,0:T(8,128)} %fusion.6, bf16[128,4096]{1,0:T(8,128)(2,1)} %all-gather.9.cloned.1.call-done, bf16[2048,4096]{0,1:T(8,128)(2,1)} %bitcast.6), kind=kOutput, calls=%fused_computation.14 | convolution fusion | flops 2147483648 | bytes 18874368 | tf_op jit(solution)/shard_map/dot_general | solution.py:32
  357.8 9.5 %fusion.4 = f32[1,2048,768]{1,2,0:T(8,128)} fusion(f32[1,2048,768]{1,2,0:T(8,128)} %fusion.5, bf16[128,4096]{1,0:T(8,128)(2,1)} %all-gather.11.cloned.1.call-done, bf16[2048,4096]{0,1:T(8,128)(2,1)} %bitcast.6), kind=kOutput, calls=%fused_computation.12 | convolution fusion | flops 2147483648 | bytes 18874368 | tf_op jit(solution)/shard_map/dot_general | solution.py:32
  367.3 9.4 %fusion.3 = f32[1,2048,768]{1,2,0:T(8,128)} fusion(f32[1,2048,768]{1,2,0:T(8,128)} %fusion.4, bf16[128,4096]{1,0:T(8,128)(2,1)} %all-gather.13.cloned.1.call-done, bf16[2048,4096]{0,1:T(8,128)(2,1)} %bitcast.6), kind=kOutput, calls=%fused_computation.10 | convolution fusion | flops 2147483648 | bytes 18874368 | tf_op jit(solution)/shard_map/dot_general | solution.py:32
  376.7 9.4 %fusion.2 = f32[1,2048,768]{1,2,0:T(8,128)} fusion(f32[1,2048,768]{1,2,0:T(8,128)} %fusion.3, bf16[128,4096]{1,0:T(8,128)(2,1)} %all-gather.15.cloned.1.call-done, bf16[2048,4096]{0,1:T(8,128)(2,1)} %bitcast.6), kind=kOutput, calls=%fused_computation.8 | convolution fusion | flops 2147483648 | bytes 18874368 | tf_op jit(solution)/shard_map/dot_general | solution.py:32
  386.2 9.7 %fusion.1 = f32[1,2048,768]{1,2,0:T(8,128)} fusion(f32[1,2048,768]{1,2,0:T(8,128)} %fusion.2, bf16[128,4096]{1,0:T(8,128)(2,1)} %all-gather.17.cloned.1.call-done, bf16[2048,4096]{0,1:T(8,128)(2,1)} %bitcast.6), kind=kOutput, calls=%fused_computation.6 | convolution fusion | flops 2147483648 | bytes 18874368 | tf_op jit(solution)/shard_map/dot_general | solution.py:32
  395.8 6.6 %broadcast_multiply_fusion = f32[1,2048,768]{1,2,0:T(8,128)} fusion(f32[1,2048,768]{1,2,0:T(8,128)} %fusion.1), kind=kLoop, calls=%fused_computation.4 | loop fusion | flops 1572864 | bytes 12582912 | tf_op jit(solution)/shard_map/mul | solution.py:36
  402.4 6.6 %copy.10 = f32[1,2048,768]{2,1,0:T(8,128)} copy(f32[1,2048,768]{1,2,0:T(8,128)} %broadcast_multiply_fusion) | data formatting | bytes 12582912 | tf_op jit(solution)/shard_map/mul | solution.py:36
  (17 shorter events, 0.2 us)
Async XLA Ops:
  87.6 22.4 %copy-start = (s32[1,8192]{1,0:T(1,128)S(1)}, s32[1,8192]{1,0:T(1,128)}, u32[]{:S(2)}) copy-start(s32[1,8192]{1,0:T(1,128)} %param.7) | copy-start | bytes 98308
  125.0 7.2 %copy-start.1 = (s32[6]{0:T(128)S(1)}, s32[6]{0:T(128)}, u32[]{:S(2)}) copy-start(s32[6]{0:T(128)} %param.9) | copy-start | bytes 76
  125.0 213.9 %all-to-all-start = ((bf16[4,2048,1024]{1,2,0:T(8,128)(2,1)}), bf16[4,2048,1024]{1,2,0:T(8,128)(2,1)}, u32[]{:S(2)}, u32[]{:S(2)}) async-start(bf16[4,2048,1024]{1,2,0:T(8,128)(2,1)} %broadcast_select_fusion), calls=%async_computation | async-start | bytes 33554432 | tf_op jit(solution)/shard_map/all_to_all | solution.py:27
  132.1 99.9 %all-reduce.3.cloned.1.call-start = ((), (), s32[]{:S(2)}) async-start(), calls=%async_computation.7 | async-start | bytes 3145728 | tf_op jit(solution)/shard_map/psum | solution.py:9
  138.8 116.2 %all-gather.7.cloned.1.call-start = ((), (), s32[]{:S(2)}) async-start(), calls=%async_computation.1 | async-start | bytes 1310720 | tf_op jit(solution)/shard_map/all_gather | solution.py:15
  232.0 116.3 %all-gather.9.cloned.1.call-start = ((), (), s32[]{:S(2)}) async-start(), calls=%async_computation.2 | async-start | bytes 1310720 | tf_op jit(solution)/shard_map/all_gather | solution.py:15
  232.7 125.1 %all-gather.11.cloned.1.call-start = ((), (), s32[]{:S(2)}) async-start(), calls=%async_computation.3 | async-start | bytes 1310720 | tf_op jit(solution)/shard_map/all_gather | solution.py:15
  233.3 134.0 %all-gather.13.cloned.1.call-start = ((), (), s32[]{:S(2)}) async-start(), calls=%async_computation.4 | async-start | bytes 1310720 | tf_op jit(solution)/shard_map/all_gather | solution.py:15
  233.9 142.8 %all-gather.15.cloned.1.call-start = ((), (), s32[]{:S(2)}) async-start(), calls=%async_computation.5 | async-start | bytes 1310720 | tf_op jit(solution)/shard_map/all_gather | solution.py:15
  234.5 151.7 %all-gather.17.cloned.1.call-start = ((), (), s32[]{:S(2)}) async-start(), calls=%async_computation.6 | async-start | bytes 1310720 | tf_op jit(solution)/shard_map/all_gather | solution.py:15
Sparse Core Ops, SparseCore 0:
  138.9 93.0 all-reduce.2
  233.5 21.3 all-gather.6
  256.6 22.3 all-gather.8
  280.4 22.4 all-gather.10
  304.3 22.4 all-gather.12
  328.1 17.0 all-gather.14
  346.8 17.7 all-gather.16
where the time goes:
time: 418 us; the launch traced here: 416 us
  waiting for transfers between devices  200 us (48%)
  local copies, waits for them, and re-layouts  91.9 us (22%)
  matrix products  56.9 us (14%)
  other arithmetic  42.4 us (10%)
  between operations  17.3 us (4%)
  starting transfers between devices  7.55 us (2%)
    psum x1, waiting for transfers between devices, from_root(): return lax.psum(jnp.where(mine, shard, jnp.zeros_like(shard)), axis)  93.2 us
    all_to_all x1, waiting for transfers between devices, per_device(): lax.all_to_all(ordered, 'ckpt', split_axis=0, concat_axis=1, tiled=True)  83.9 us
    gather x2, local copies, waits for them, and re-layouts, per_device(): ordered = jnp.take(feats, example_ids[0], axis=0)  70.4 us
    dot_general x6, matrix products, per_device(): lax.dot_general(resident, chosen, contract, preferred_element_type=jnp.fl...  56.9 us
    all_gather x6, waiting for transfers between devices, fetch(): return lax.all_gather(got, 'ckpt', axis=1, tiled=True)  19.8 us
    convert_element_type x1, other arithmetic, per_device(): (codes[0, 0].astype(jnp.float32) * jnp.repeat(scales[0, 0], block, axis=-...  18 us
    select_n x2, other arithmetic, per_device(): ordered = jnp.take(feats, example_ids[0], axis=0)  15 us
    broadcast_in_dim x1, local copies, waits for them, and re-layouts, per_device(): jnp.repeat(scales[0, 0], block, axis=-1)  10.3 us
  transfers between devices with their start and end apart: 8, of which 3 were waited for; matrix products, arithmetic and copies ran while one was open for 12% of the time, Pallas kernels for 0%

commit v1 on v0

v1 whole, which is shorter than its diff:
```python
import jax
import jax.numpy as jnp
from jax import lax
from jax.sharding import PartitionSpec as P

PIECES = 4


def swap(value, distance, size):
    return lax.ppermute(value, "ckpt", [(i, i ^ distance) for i in range(size)])


def per_device(codes, scales, example_ids, targets, owners):
    me = lax.axis_index("ckpt")
    size = lax.axis_size("ckpt")
    width = codes.shape[-1]
    blocks = scales.shape[-1]
    block = width // blocks
    per_owner = targets.shape[0]
    rounds = owners.shape[0]
    rows = codes.shape[2]
    own_rows = rows // size
    piece_rows = own_rows // PIECES

    piece = lax.dynamic_slice_in_dim(targets, me * width, width, 1)
    everyone = lax.all_gather(piece, "wide", axis=0)
    chosen = jnp.take(everyone, owners, axis=0).reshape(rounds * per_owner, width)

    feats = (codes[0, 0].astype(jnp.float32) * jnp.repeat(scales[0, 0], block, axis=-1)).astype(
        jnp.bfloat16
    )
    ordered = jnp.take(feats, example_ids[0], axis=0, mode="clip", unique_indices=True)
    ordered = ordered.reshape(size, PIECES, piece_rows, width)
    contract = (((1,), (1,)), ((), ()))

    def partial(home, step):
        part = lax.dynamic_index_in_dim(ordered[:, step], home, 0, keepdims=False)
        return lax.dot_general(part, chosen, contract, preferred_element_type=jnp.float32)

    factor = 1.0 / size
    pieces = []
    for step in range(PIECES):
        far_pair = partial(me ^ 3, step).astype(jnp.bfloat16)
        near_pair = partial(me ^ 1, step).astype(jnp.bfloat16)
        far = partial(me ^ 2, step) + swap(far_pair, 1, size).astype(jnp.float32)
        near = partial(me, step) + swap(near_pair, 1, size).astype(jnp.float32)
        total = near + swap(far.astype(jnp.bfloat16), 2, size).astype(jnp.float32)
        pieces.append(total * factor)
    return jnp.concatenate(pieces, axis=0)[None]


def solution(mesh):
    return jax.shard_map(
        per_device,
        mesh=mesh,
        in_specs=(
            P("ckpt", "wide", None, None),
            P("ckpt", "wide", None, None),
            P("wide", None),
            P("wide", None),
            P(),
        ),
        out_specs=P("wide", "ckpt", None),
        check_vma=False,
    )
```

time: 418 us -> 220 us (0.53)
  waiting for transfers between devices: 200 us -> 59.8 us
  matrix products: 56.9 us -> 18 us
  other arithmetic: 42.4 us -> 30.6 us
    psum x1 -> x0, waiting for transfers between devices: 93.2 us -> none  [from_root(): return lax.psum(jnp.where(mine, shard, jnp.zeros_like(shard)), axis)]
    all_to_all x1 -> x0, waiting for transfers between devices: 83.9 us -> none  [per_device(): lax.all_to_all(ordered, 'ckpt', split_axis=0, concat_axis=1, tiled=True)]
    ppermute x0 -> x12, waiting for transfers between devices: none -> 59.8 us  [swap(): return lax.ppermute(value, 'ckpt', [(i, i ^ distance) for i in range(size)])]
    dot_general x6 -> x16, matrix products: 56.9 us -> 18 us  [partial(): lax.dot_general(part, chosen, contract, preferred_element_type=jnp.float32)]
    all_gather x6 -> x1, waiting for transfers between devices: 19.8 us -> 0.01 us  [per_device(): everyone = lax.all_gather(piece, 'wide', axis=0)]
    gather x2, local copies, waits for them, and re-layouts: 70.4 us -> 50.7 us  [the longest x1 48.4 us: per_device(): jnp.take(feats, example_ids[0], axis=0, mode='clip', unique_indices=True)]
    select_n x3 -> x2, other arithmetic: 17.2 us -> 0.22 us  [per_device(): jnp.take(everyone, owners, axis=0).reshape(rounds * per_owner, width)]
    slice x1, local copies, waits for them, and re-layouts: 0.67 us -> 12.3 us  [partial(): part = lax.dynamic_index_in_dim(ordered[:, step], home, 0, keepdims=False)]
  transfers between devices with their start and end apart: 8 -> 13, of which waited for: 3 -> 4; matrix products, arithmetic and copies ran while one was open for 12% -> 53% of each run, Pallas kernels for 0% -> 0%
where the time goes in v1:
time: 220 us; the launch traced here: 219 us
  local copies, waits for them, and re-layouts  88.1 us (40%)
  waiting for transfers between devices  59.8 us (27%)
  other arithmetic  30.6 us (14%)
  matrix products  18 us (8%)
  between operations  13.7 us (6%)
  starting transfers between devices  9.22 us (4%)
    ppermute x12, waiting for transfers between devices, swap(): return lax.ppermute(value, 'ckpt', [(i, i ^ distance) for i in range(size)])  59.8 us
    gather x1, local copies, waits for them, and re-layouts, per_device(): jnp.take(feats, example_ids[0], axis=0, mode='clip', unique_indices=True)  48.4 us
    convert_element_type x1, other arithmetic, per_device(): (codes[0, 0].astype(jnp.float32) * jnp.repeat(scales[0, 0], block, axis=-...  26.2 us
    dot_general x16, matrix products, partial(): lax.dot_general(part, chosen, contract, preferred_element_type=jnp.float32)  18 us
    broadcast_in_dim x1, local copies, waits for them, and re-layouts, per_device(): jnp.repeat(scales[0, 0], block, axis=-1)  17.1 us
    slice x1, local copies, waits for them, and re-layouts, partial(): part = lax.dynamic_index_in_dim(ordered[:, step], home, 0, keepdims=False)  12.3 us
    ppermute x12, starting transfers between devices, swap(): return lax.ppermute(value, 'ckpt', [(i, i ^ distance) for i in range(size)])  9.22 us
  transfers between devices with their start and end apart: 13, of which 4 were waited for; matrix products, arithmetic and copies ran while one was open for 53% of the time, Pallas kernels for 0%

profile of v1, /device:TPU:0, one launch (start us, length us, event | category | flops | bytes accessed | tf_op | source)
XLA Modules:
  0.0 219.4 jit_solution(8367899937948625915)
XLA Ops:
  6.5 1.2 copy-done
  8.6 3.5 %copy.6 = f32[8192,8]{1,0:T(8,128)} copy(f32[8192,8]{0,1:T(8,128)} %bitcast.106) | data formatting | bytes 524288 | tf_op jit(solution)/shard_map/squeeze | solution.py:29
  12.1 17.1 %broadcast_in_dim.22 = f32[8192,8,128]{2,1,0:T(8,128)} broadcast(f32[8192,8]{1,0:T(8,128)} %copy.6), dimensions={0,1} | broadcast | bytes 33816576 | tf_op jit(solution)/shard_map/broadcast_in_dim | solution.py:29
  29.2 26.2 %fusion = bf16[8192,1024]{1,0:T(8,128)(2,1)} fusion(f32[1024,8,8,128]{3,2,1,0:T(8,128)} %bitcast.87, bf16[1,1,8192,1024]{3,2,1,0:T(8,128)(2,1)} %param.5), kind=kLoop, calls=%fused_computation.3 | loop fusion | flops 25165824 | bytes 67108864 | tf_op jit(solution)/shard_map/convert_element_type | solution.py:29
  55.4 48.4 %gather_fusion = bf16[8192,1024]{1,0:T(8,128)(2,1)} fusion(bf16[8192,1024]{1,0:T(8,128)(2,1)} %fusion, s32[8192]{0:T(1024)S(1)} %broadcast_clamp_fusion), kind=kCustom, calls=%fused_computation | custom fusion | bytes 33587200 | tf_op jit(solution)/shard_map/jit(_take)/gather | solution.py:32
  103.8 12.3 %fusion.65 = (bf16[4,1,512,1024]{3,2,1,0:T(8,128)(2,1)}, bf16[4,1,512,1024]{3,2,1,0:T(8,128)(2,1)}, bf16[4,1,512,1024]{3,2,1,0:T(8,128)(2,1)}, bf16[4,1,512,1024]{3,2,1,0:T(8,128)(2,1)}) fusion(bf16[4,4,512,1024]{3,2,1,0:T(8,128)(2,1)} %bitcast.88), kind=kLoop, calls=%fused_computation.83 | loop fusion | bytes 33554432 | tf_op jit(solution)/shard_map/slice | solution.py:37
  116.2 2.2 %gather_fusion.1 = bf16[6,128,1024]{2,1,0:T(8,128)(2,1)S(1)} fusion(bf16[8,128,1024]{2,1,0:T(8,128)(2,1)} %bitcast.105, s32[1024]{0:T(1024)S(1)} %pad_clamp_fusion), kind=kCustom, calls=%fused_computation.1 | custom fusion | bytes 3145752 | tf_op jit(solution)/shard_map/jit(_take)/gather | solution.py:27
  118.6 2.4 %convolution_convert_fusion = bf16[512,768]{1,0:T(8,128)(2,1)S(1)} fusion(bf16[768,1024]{1,0:T(8,128)(2,1)S(1)} %bitcast.89, bf16[4,1,512,1024]{3,2,1,0:T(8,128)(2,1)} %get-tuple-element.6, s32[]{:T(128)S(6)} %select_n.114), kind=kOutput, calls=%fused_computation.14 | convolution fusion | flops 805699584 | bytes 3407876 | tf_op jit(solution)/shard_map/dot_general | solution.py:38
  121.1 1.0 fusion.7
  122.2 1.2 copy-done.4
  123.3 1.0 convolution_convert_fusion.2
  124.4 1.0 fusion.15
  125.4 1.0 convolution_convert_fusion.1
  126.4 1.0 convolution_convert_fusion.3
  127.5 1.1 copy-done.3
  128.6 1.0 convolution_convert_fusion.4
  129.7 1.0 fusion.23
  131.8 1.0 fusion.31
  132.9 1.0 convolution_convert_fusion.5
  133.9 1.0 convolution_convert_fusion.6
  134.9 1.0 convolution_convert_fusion.7
  137.0 1.0 add_convert_fusion
  138.1 2.6 %collective-permute-start.11 = (bf16[512,768]{1,0:T(8,128)(2,1)S(1)}, bf16[512,768]{1,0:T(8,128)(2,1)S(1)}, u32[]{:S(2)}, u32[]{:S(2)}) collective-permute-start(bf16[512,768]{1,0:T(8,128)(2,1)S(1)} %add_convert_fusion), channel_id=1, source_target_pairs={{0,16},{8,24},{16,0},{24,8},{1,17},{9,25},{17,1},{25,9},{2,18},{10... | collective-permute-start | bytes 2359304 | tf_op jit(solution)/shard_map/ppermute | solution.py:10
  140.7 1.2 add_convert_fusion.1
  142.0 1.0 add_convert_fusion.2
  143.3 1.9 collective-permute-start.5
  146.5 12.6 %collective-permute-done.11 = bf16[512,768]{1,0:T(8,128)(2,1)S(1)} collective-permute-done((bf16[512,768]{1,0:T(8,128)(2,1)S(1)}, bf16[512,768]{1,0:T(8,128)(2,1)S(1)}, u32[]{:S(2)}, u32[]{:S(2)}) %collective-permute-start.11) | collective-permute-done | bytes 786464 | tf_op jit(solution)/shard_map/ppermute | solution.py:10
  159.1 2.0 collective-permute-start.2
  161.5 14.5 %collective-permute-done.8 = bf16[512,768]{1,0:T(8,128)(2,1)S(1)} collective-permute-done((bf16[512,768]{1,0:T(8,128)(2,1)S(1)}, bf16[512,768]{1,0:T(8,128)(2,1)S(1)}, u32[]{:S(2)}, u32[]{:S(2)}) %collective-permute-start.8) | collective-permute-done | bytes 786464 | tf_op jit(solution)/shard_map/ppermute | solution.py:10
  176.3 16.5 %collective-permute-done.5 = bf16[512,768]{1,0:T(8,128)(2,1)S(1)} collective-permute-done((bf16[512,768]{1,0:T(8,128)(2,1)S(1)}, bf16[512,768]{1,0:T(8,128)(2,1)S(1)}, u32[]{:S(2)}, u32[]{:S(2)}) %collective-permute-start.5) | collective-permute-done | bytes 786464 | tf_op jit(solution)/shard_map/ppermute | solution.py:10
  193.1 16.2 %collective-permute-done.2 = bf16[512,768]{1,0:T(8,128)(2,1)S(1)} collective-permute-done((bf16[512,768]{1,0:T(8,128)(2,1)S(1)}, bf16[512,768]{1,0:T(8,128)(2,1)S(1)}, u32[]{:S(2)}, u32[]{:S(2)}) %collective-permute-start.2) | collective-permute-done | bytes 786464 | tf_op jit(solution)/shard_map/ppermute | solution.py:10
  209.7 2.9 %maximum_bitcast_fusion = f32[1,2048,768]{2,1,0:T(8,128)} fusion(f32[512,768]{1,0:T(8,128)S(1)} %add_multiply_fusion, f32[512,768]{1,0:T(8,128)S(1)} %add_multiply_fusion.1, f32[512,768]{1,0:T(8,128)S(1)} %add_multiply_fusion.2, f32[512,768]{1,0:T(8,128)S(1)} %add_multiply_fusion.3), kind=kLoop, calls=%fused_computation.4 | loop fusion | flops 4718592 | bytes 12582912 | tf_op jit(solution)/shard_map/broadcast_in_dim | solution.py:49
  (44 shorter events, 6.2 us)
Async XLA Ops:
  6.5 1.2 copy-start
  6.5 109.6 %all-gather.3.cloned.1.call-start = ((), (), s32[]{:S(2)}) async-start(), calls=%async_computation | async-start | bytes 2359296 | tf_op jit(solution)/shard_map/all_gather | solution.py:26
  8.5 3.5 %copy-start.6 = (s32[1,8192]{1,0:T(1,128)S(1)}, s32[1,8192]{1,0:T(1,128)}, u32[]{:S(2)}) copy-start(s32[1,8192]{1,0:T(1,128)} %param.7) | copy-start | bytes 98308
  55.4 48.4 %copy-start.7 = (s32[6]{0:T(128)S(1)}, s32[6]{0:T(128)}, u32[]{:S(2)}) copy-start(s32[6]{0:T(128)} %param.9) | copy-start | bytes 76
  118.6 2.5 %copy-start.5 = (bf16[4,1,512,1024]{3,2,1,0:T(8,128)(2,1)S(1)}, bf16[4,1,512,1024]{3,2,1,0:T(8,128)(2,1)}, u32[]{:S(2)}) copy-start(bf16[4,1,512,1024]{3,2,1,0:T(8,128)(2,1)} %get-tuple-element.6) | copy-start | bytes 12582916
  121.1 2.2 copy-start.4
  126.4 2.2 copy-start.3
  129.6 2.2 copy-start.2
  130.7 5.9 %collective-permute-start.10 = (bf16[512,768]{1,0:T(8,128)(2,1)S(1)}, bf16[512,768]{1,0:T(8,128)(2,1)S(1)}, u32[]{:S(2)}, u32[]{:S(2)}) collective-permute-start(bf16[512,768]{1,0:T(8,128)(2,1)S(1)} %convolution_convert_fusion), channel_id=1, source_target_pairs={{0,8},{8,0},{16,24},{24,16},{1,9},{9,1},{17,25},{25,17},{2,10},{10... | collective-permute-start | bytes 2359304 | tf_op jit(solution)/shard_map/ppermute | solution.py:10
  131.2 6.8 %collective-permute-start.7 = (bf16[512,768]{1,0:T(8,128)(2,1)S(1)}, bf16[512,768]{1,0:T(8,128)(2,1)S(1)}, u32[]{:S(2)}, u32[]{:S(2)}) collective-permute-start(bf16[512,768]{1,0:T(8,128)(2,1)S(1)} %convolution_convert_fusion.2), channel_id=1, source_target_pairs={{0,8},{8,0},{16,24},{24,16},{1,9},{9,1},{17,25},{25,17},{2,10},{10... | collective-permute-start | bytes 2359304 | tf_op jit(solution)/shard_map/ppermute | solution.py:10
  131.3 10.6 %collective-permute-start.4 = (bf16[512,768]{1,0:T(8,128)(2,1)S(1)}, bf16[512,768]{1,0:T(8,128)(2,1)S(1)}, u32[]{:S(2)}, u32[]{:S(2)}) collective-permute-start(bf16[512,768]{1,0:T(8,128)(2,1)S(1)} %convolution_convert_fusion.4), channel_id=1, source_target_pairs={{0,8},{8,0},{16,24},{24,16},{1,9},{9,1},{17,25},{25,17},{2,10},{10... | collective-permute-start | bytes 2359304 | tf_op jit(solution)/shard_map/ppermute | solution.py:10
  136.0 7.1 %collective-permute-start.9 = (bf16[512,768]{1,0:T(8,128)(2,1)S(1)}, bf16[512,768]{1,0:T(8,128)(2,1)S(1)}, u32[]{:S(2)}, u32[]{:S(2)}) collective-permute-start(bf16[512,768]{1,0:T(8,128)(2,1)S(1)} %convolution_convert_fusion.1), channel_id=1, source_target_pairs={{0,8},{8,0},{16,24},{24,16},{1,9},{9,1},{17,25},{25,17},{2,10},{10... | collective-permute-start | bytes 2359304 | tf_op jit(solution)/shard_map/ppermute | solution.py:10
  136.5 9.8 %collective-permute-start.6 = (bf16[512,768]{1,0:T(8,128)(2,1)S(1)}, bf16[512,768]{1,0:T(8,128)(2,1)S(1)}, u32[]{:S(2)}, u32[]{:S(2)}) collective-permute-start(bf16[512,768]{1,0:T(8,128)(2,1)S(1)} %convolution_convert_fusion.3), channel_id=1, source_target_pairs={{0,8},{8,0},{16,24},{24,16},{1,9},{9,1},{17,25},{25,17},{2,10},{10... | collective-permute-start | bytes 2359304 | tf_op jit(solution)/shard_map/ppermute | solution.py:10
  136.6 6.7 %collective-permute-start.1 = (bf16[512,768]{1,0:T(8,128)(2,1)S(1)}, bf16[512,768]{1,0:T(8,128)(2,1)S(1)}, u32[]{:S(2)}, u32[]{:S(2)}) collective-permute-start(bf16[512,768]{1,0:T(8,128)(2,1)S(1)} %convolution_convert_fusion.6), channel_id=1, source_target_pairs={{0,8},{8,0},{16,24},{24,16},{1,9},{9,1},{17,25},{25,17},{2,10},{10... | collective-permute-start | bytes 2359304 | tf_op jit(solution)/shard_map/ppermute | solution.py:10
  138.1 21.0 %collective-permute-start.11 = (bf16[512,768]{1,0:T(8,128)(2,1)S(1)}, bf16[512,768]{1,0:T(8,128)(2,1)S(1)}, u32[]{:S(2)}, u32[]{:S(2)}) collective-permute-start(bf16[512,768]{1,0:T(8,128)(2,1)S(1)} %add_convert_fusion), channel_id=1, source_target_pairs={{0,16},{8,24},{16,0},{24,8},{1,17},{9,25},{17,1},{25,9},{2,18},{10... | collective-permute-start | bytes 2359304 | tf_op jit(solution)/shard_map/ppermute | solution.py:10
  141.9 34.0 %collective-permute-start.8 = (bf16[512,768]{1,0:T(8,128)(2,1)S(1)}, bf16[512,768]{1,0:T(8,128)(2,1)S(1)}, u32[]{:S(2)}, u32[]{:S(2)}) collective-permute-start(bf16[512,768]{1,0:T(8,128)(2,1)S(1)} %add_convert_fusion.1), channel_id=1, source_target_pairs={{0,16},{8,24},{16,0},{24,8},{1,17},{9,25},{17,1},{25,9},{2,18},{10... | collective-permute-start | bytes 2359304 | tf_op jit(solution)/shard_map/ppermute | solution.py:10
  143.1 33.2 %collective-permute-start.3 = (bf16[512,768]{1,0:T(8,128)(2,1)S(1)}, bf16[512,768]{1,0:T(8,128)(2,1)S(1)}, u32[]{:S(2)}, u32[]{:S(2)}) collective-permute-start(bf16[512,768]{1,0:T(8,128)(2,1)S(1)} %convolution_convert_fusion.5), channel_id=1, source_target_pairs={{0,8},{8,0},{16,24},{24,16},{1,9},{9,1},{17,25},{25,17},{2,10},{10... | collective-permute-start | bytes 2359304 | tf_op jit(solution)/shard_map/ppermute | solution.py:10
  143.3 49.5 %collective-permute-start.5 = (bf16[512,768]{1,0:T(8,128)(2,1)S(1)}, bf16[512,768]{1,0:T(8,128)(2,1)S(1)}, u32[]{:S(2)}, u32[]{:S(2)}) collective-permute-start(bf16[512,768]{1,0:T(8,128)(2,1)S(1)} %add_convert_fusion.2), channel_id=1, source_target_pairs={{0,16},{8,24},{16,0},{24,8},{1,17},{9,25},{17,1},{25,9},{2,18},{10... | collective-permute-start | bytes 2359304 | tf_op jit(solution)/shard_map/ppermute | solution.py:10
  146.3 46.9 %collective-permute-start = (bf16[512,768]{1,0:T(8,128)(2,1)S(1)}, bf16[512,768]{1,0:T(8,128)(2,1)S(1)}, u32[]{:S(2)}, u32[]{:S(2)}) collective-permute-start(bf16[512,768]{1,0:T(8,128)(2,1)S(1)} %convolution_convert_fusion.7), channel_id=1, source_target_pairs={{0,8},{8,0},{16,24},{24,16},{1,9},{9,1},{17,25},{25,17},{2,10},{10... | collective-permute-start | bytes 2359304 | tf_op jit(solution)/shard_map/ppermute | solution.py:10
  159.1 50.3 %collective-permute-start.2 = (bf16[512,768]{1,0:T(8,128)(2,1)S(1)}, bf16[512,768]{1,0:T(8,128)(2,1)S(1)}, u32[]{:S(2)}, u32[]{:S(2)}) collective-permute-start(bf16[512,768]{1,0:T(8,128)(2,1)S(1)} %add_convert_fusion.3), channel_id=1, source_target_pairs={{0,16},{8,24},{16,0},{24,8},{1,17},{9,25},{17,1},{25,9},{2,18},{10... | collective-permute-start | bytes 2359304 | tf_op jit(solution)/shard_map/ppermute | solution.py:10
  209.6 2.9 %copy-start.1 = (bf16[128,4096]{1,0:T(8,128)(2,1)S(1)}, bf16[128,4096]{1,0:T(8,128)(2,1)}, u32[]{:S(2)}) copy-start(bf16[128,4096]{1,0:T(8,128)(2,1)} %param.8) | copy-start | bytes 3145732
Sparse Core Ops, SparseCore 0:
  9.5 51.7 all-gather.2

commit v2 on v1

--- a/solution.py
+++ b/solution.py
@@ -1,9 +1,77 @@
+import functools
+
 import jax
 import jax.numpy as jnp
 from jax import lax
+from jax.experimental import pallas as pl
+from jax.experimental.pallas import tpu as pltpu
 from jax.sharding import PartitionSpec as P
 
 PIECES = 4
+TILE_ROWS = 512
+UNROLL = 32
+
+
+def order_kernel(tiles, ids_ref, codes_ref, scales_ref, out_ref, feats, picked):
+    step = pl.program_id(0)
+    tile_rows, width = codes_ref.shape
+    blocks = scales_ref.shape[1]
+    block = width // blocks
+
+    @pl.when(step < tiles)
+    def scale():
+        first = step * (tile_rows * blocks)
+        for q in range(blocks):
+            codes = codes_ref[:, q * block : (q + 1) * block].astype(jnp.float32)
+            value = (codes * scales_ref[:, q : q + 1]).astype(jnp.bfloat16)
+            feats[pl.ds(first + q, tile_rows, stride=blocks), :] = value.astype(jnp.float32)
+
+    @pl.when(step >= tiles)
+    def order():
+        base = (step - tiles) * tile_rows
+
+        def some(i, carry):
+            at = i * UNROLL
+            rows = [
+                feats[pl.ds(pl.multiple_of(ids_ref[base + at + u] * blocks, blocks), blocks), :]
+                for u in range(UNROLL)
+            ]
+            for u in range(UNROLL):
+                to = pl.multiple_of((at + u) * blocks, blocks)
+                picked[pl.ds(to, blocks), :] = rows[u]
+            return carry
+
+        lax.fori_loop(0, tile_rows // UNROLL, some, 0)
+        for q in range(blocks):
+            out_ref[:, q * block : (q + 1) * block] = picked[
+                pl.ds(q, tile_rows, stride=blocks), :
+            ].astype(out_ref.dtype)
+
+
+def order_rows(codes, scales, ids):
+    rows, width = codes.shape
+    blocks = scales.shape[1]
+    block = width // blocks
+    tiles = rows // TILE_ROWS
+    return pl.pallas_call(
+        functools.partial(order_kernel, tiles),
+        grid=(2 * tiles,),
+        in_specs=[
+            pl.BlockSpec(memory_space=pltpu.SMEM),
+            pl.BlockSpec((TILE_ROWS, width), lambda s: (jnp.minimum(s, tiles - 1), 0)),
+            pl.BlockSpec((TILE_ROWS, blocks), lambda s: (jnp.minimum(s, tiles - 1), 0)),
+        ],
+        out_specs=pl.BlockSpec((TILE_ROWS, width), lambda s: (jnp.maximum(s - tiles, 0), 0)),
+        out_shape=jax.ShapeDtypeStruct((rows, width), jnp.bfloat16),
+        scratch_shapes=[
+            pltpu.VMEM((rows * blocks, block), jnp.float32),
+            pltpu.VMEM((TILE_ROWS * blocks, block), jnp.float32),
+        ],
+        compiler_params=pltpu.CompilerParams(vmem_limit_bytes=50 * 2**20),
+        cost_estimate=pl.CostEstimate(
+            flops=rows * width * 100, bytes_accessed=rows * width * 8, transcendentals=0
+        ),
+    )(ids, codes, scales)
 
 
 def swap(value, distance, size):
@@ -14,8 +82,6 @@
     me = lax.axis_index("ckpt")
     size = lax.axis_size("ckpt")
     width = codes.shape[-1]
-    blocks = scales.shape[-1]
-    block = width // blocks
     per_owner = targets.shape[0]
     rounds = owners.shape[0]
     rows = codes.shape[2]
@@ -26,15 +92,11 @@
     everyone = lax.all_gather(piece, "wide", axis=0)
     chosen = jnp.take(everyone, owners, axis=0).reshape(rounds * per_owner, width)
 
-    feats = (codes[0, 0].astype(jnp.float32) * jnp.repeat(scales[0, 0], block, axis=-1)).astype(
-        jnp.bfloat16
-    )
-    ordered = jnp.take(feats, example_ids[0], axis=0, mode="clip", unique_indices=True)
-    ordered = ordered.reshape(size, PIECES, piece_rows, width)
+    ordered = order_rows(codes[0, 0], scales[0, 0], example_ids[0])
     contract = (((1,), (1,)), ((), ()))
 
     def partial(home, step):
-        part = lax.dynamic_index_in_dim(ordered[:, step], home, 0, keepdims=False)
+        part = lax.dynamic_slice_in_dim(ordered, home * own_rows + step * piece_rows, piece_rows, 0)
         return lax.dot_general(part, chosen, contract, preferred_element_type=jnp.float32)
 
     factor = 1.0 / size

time: 220 us -> 164 us (0.75)
  local copies, waits for them, and re-layouts: 88.1 us -> 7.8 us
  Pallas kernels: 0 us -> 37.8 us
  other arithmetic: 30.6 us -> 4.38 us
  waiting for transfers between devices: 59.8 us -> 72.3 us
  matrix products: 18 us -> 21.1 us
  starting transfers between devices: 9.22 us -> 6.84 us
    gather x1 -> x0, local copies, waits for them, and re-layouts: 48.4 us -> none  [per_device(): jnp.take(feats, example_ids[0], axis=0, mode='clip', unique_indices=True)]
    pallas_call x0 -> x1, Pallas kernels: none -> 37.8 us  [order_rows(): pl.pallas_call(functools.partial(order_kernel, tiles), grid=(2 * tiles,),...]
    convert_element_type x1 -> x0, other arithmetic: 26.2 us -> none  [per_device(): (codes[0, 0].astype(jnp.float32) * jnp.repeat(scales[0, 0], block, axis=-...]
    broadcast_in_dim x1, local copies, waits for them, and re-layouts: 17.1 us -> 0.07 us  [per_device(): jnp.take(everyone, owners, axis=0).reshape(rounds * per_owner, width)]
    slice x1 -> x0, local copies, waits for them, and re-layouts: 12.3 us -> none  [partial(): part = lax.dynamic_index_in_dim(ordered[:, step], home, 0, keepdims=False)]
    all_gather x1, waiting for transfers between devices: 0.01 us -> 11.3 us  [per_device(): everyone = lax.all_gather(piece, 'wide', axis=0)]
    squeeze x1 -> x0, local copies, waits for them, and re-layouts: 3.53 us -> none  [per_device(): scales[0, 0]]
    dot_general x16, matrix products: 18 us -> 21.1 us  [partial(): lax.dot_general(part, chosen, contract, preferred_element_type=jnp.float32)]
  transfers between devices with their start and end apart: 13 -> 13, of which waited for: 4 -> 5; matrix products, arithmetic and copies ran while one was open for 53% -> 14% of each run, Pallas kernels for 0% -> 23%
where the time goes in v2:
time: 164 us
  waiting for transfers between devices  72.3 us (44%)
  Pallas kernels  37.8 us (23%)
  matrix products  21.1 us (13%)
  between operations  13.7 us (8%)
  local copies, waits for them, and re-layouts  7.8 us (5%)
  starting transfers between devices  6.84 us (4%)
  other arithmetic  4.38 us (3%)
    ppermute x12, waiting for transfers between devices, swap(): return lax.ppermute(value, 'ckpt', [(i, i ^ distance) for i in range(size)])  60.9 us
    pallas_call x1, Pallas kernels, order_rows(): pl.pallas_call(functools.partial(order_kernel, tiles), grid=(2 * tiles,),...  37.8 us
    dot_general x16, matrix products, partial(): lax.dot_general(part, chosen, contract, preferred_element_type=jnp.float32)  21.1 us
    all_gather x1, waiting for transfers between devices, per_device(): everyone = lax.all_gather(piece, 'wide', axis=0)  11.3 us
    ppermute x12, starting transfers between devices, swap(): return lax.ppermute(value, 'ckpt', [(i, i ^ distance) for i in range(size)])  6.84 us
    unnamed x11, local copies, waits for them, and re-layouts  4.77 us
  transfers between devices with their start and end apart: 13, of which 5 were waited for; matrix products, arithmetic and copies ran while one was open for 14% of the time, Pallas kernels for 23%

profile of v2, /device:TPU:0, one launch (start us, length us, event | category | flops | bytes accessed | tf_op | source)
XLA Modules:
  0.0 163.9 jit_solution(15721554701381101979)
XLA Ops:
  6.5 1.2 copy-done
  7.8 0.7 constant_dynamic-slice_fusion
  8.5 3.5 %copy.6 = f32[1,1,8192,8]{3,2,1,0:T(8,128)} copy(f32[1,1,8192,8]{2,3,1,0:T(8,128)} %param.6) | data formatting | bytes 524288 | tf_op args[1]
  12.1 37.8 %shard_map.55 = bf16[8192,1024]{1,0:T(8,128)(2,1)} custom-call(s32[8192]{0:T(1024)S(1)} %bitcast.26, bf16[8192,1024]{1,0:T(8,128)(2,1)} %bitcast.27, f32[8192,8]{1,0:T(8,128)} %bitcast.28), custom_call_target="tpu_custom_call" | custom-call | flops 838860800 | bytes 67108864 | tf_op jit(solution)/shard_map/pallas_call | solution.py:56
  50.0 11.3 %all-gather.3.cloned.1.call-done = bf16[1024,1024]{1,0:T(8,128)(2,1)} async-done(((bf16[128,1024]{1,0:T(8,128)(2,1)}), bf16[1024,1024]{1,0:T(8,128)(2,1)}) %all-gather.3.cloned.1.call-update) | async-done | bytes 2097168 | tf_op jit(solution)/shard_map/all_gather | solution.py:92
  61.3 2.2 %gather_fusion = bf16[6,128,1024]{2,1,0:T(8,128)(2,1)S(1)} fusion(bf16[8,128,1024]{2,1,0:T(8,128)(2,1)} %bitcast.29, s32[1024]{0:T(1024)S(1)} %pad_clamp_fusion), kind=kCustom, calls=%fused_computation | custom fusion | bytes 3145752 | tf_op jit(solution)/shard_map/jit(_take)/gather | solution.py:93
  63.9 2.4 %convolution_convert_fusion.6 = bf16[512,768]{1,0:T(8,128)(2,1)S(1)} fusion(bf16[768,1024]{1,0:T(8,128)(2,1)S(1)} %bitcast_select_fusion, bf16[8192,1024]{1,0:T(8,128)(2,1)} %shard_map.55, s32[]{:T(128)S(6)} %select_n.67), kind=kOutput, calls=%fused_computation.17 | convolution fusion | flops 805699584 | bytes 3407876 | tf_op jit(solution)/shard_map/dot_general | solution.py:100
  66.4 3.0 %convolution_convert_fusion.7 = bf16[512,768]{1,0:T(8,128)(2,1)S(1)} fusion(bf16[768,1024]{1,0:T(8,128)(2,1)S(1)} %bitcast_select_fusion, bf16[8192,1024]{1,0:T(8,128)(2,1)} %shard_map.55, s32[]{:T(128)S(6)} %select_n.65), kind=kOutput, calls=%fused_computation.18 | convolution fusion | flops 805699584 | bytes 3407876 | tf_op jit(solution)/shard_map/dot_general | solution.py:100
  69.5 2.3 %fusion.30 = f32[512,768]{1,0:T(8,128)S(1)} fusion(bf16[768,1024]{1,0:T(8,128)(2,1)S(1)} %bitcast_select_fusion, bf16[8192,1024]{1,0:T(8,128)(2,1)} %shard_map.55, s32[]{:T(128)S(6)} %select_n.61), kind=kOutput, calls=%fused_computation.41 | convolution fusion | flops 805306368 | bytes 4194308 | tf_op jit(solution)/shard_map/dot_general | solution.py:100
  71.7 1.0 convolution_convert_fusion.4
  73.3 1.0 convolution_convert_fusion.5
  74.4 1.0 fusion.22
  75.5 1.0 convolution_convert_fusion.2
  76.5 0.6 collective-permute-start.7
  77.0 1.0 fusion.14
  78.1 1.0 fusion.6
  79.1 1.0 convolution_convert_fusion.3
  80.1 1.0 convolution_convert_fusion
  81.2 1.0 convolution_convert_fusion.1
  82.3 1.0 add_convert_fusion.3
  83.3 1.5 collective-permute-start.2
  84.9 1.2 add_convert_fusion.2
  86.1 0.6 collective-permute-start.5
  86.7 1.0 add_convert_fusion.1
  87.8 1.5 collective-permute-start.8
  89.4 1.0 add_convert_fusion
  90.6 13.2 %collective-permute-done.2 = bf16[512,768]{1,0:T(8,128)(2,1)S(1)} collective-permute-done((bf16[512,768]{1,0:T(8,128)(2,1)S(1)}, bf16[512,768]{1,0:T(8,128)(2,1)S(1)}, u32[]{:S(2)}, u32[]{:S(2)}) %collective-permute-start.2) | collective-permute-done | bytes 786464 | tf_op jit(solution)/shard_map/ppermute | solution.py:78
  103.8 1.5 collective-permute-start.11
  105.6 15.0 %collective-permute-done.5 = bf16[512,768]{1,0:T(8,128)(2,1)S(1)} collective-permute-done((bf16[512,768]{1,0:T(8,128)(2,1)S(1)}, bf16[512,768]{1,0:T(8,128)(2,1)S(1)}, u32[]{:S(2)}, u32[]{:S(2)}) %collective-permute-start.5) | collective-permute-done | bytes 786464 | tf_op jit(solution)/shard_map/ppermute | solution.py:78
  120.9 16.6 %collective-permute-done.8 = bf16[512,768]{1,0:T(8,128)(2,1)S(1)} collective-permute-done((bf16[512,768]{1,0:T(8,128)(2,1)S(1)}, bf16[512,768]{1,0:T(8,128)(2,1)S(1)}, u32[]{:S(2)}, u32[]{:S(2)}) %collective-permute-start.8) | collective-permute-done | bytes 786464 | tf_op jit(solution)/shard_map/ppermute | solution.py:78
  137.8 16.1 %collective-permute-done.11 = bf16[512,768]{1,0:T(8,128)(2,1)S(1)} collective-permute-done((bf16[512,768]{1,0:T(8,128)(2,1)S(1)}, bf16[512,768]{1,0:T(8,128)(2,1)S(1)}, u32[]{:S(2)}, u32[]{:S(2)}) %collective-permute-start.11) | collective-permute-done | bytes 786464 | tf_op jit(solution)/shard_map/ppermute | solution.py:78
  154.2 2.9 %maximum_bitcast_fusion = f32[1,2048,768]{2,1,0:T(8,128)} fusion(f32[512,768]{1,0:T(8,128)S(1)} %add_multiply_fusion, f32[512,768]{1,0:T(8,128)S(1)} %add_multiply_fusion.1, f32[512,768]{1,0:T(8,128)S(1)} %add_multiply_fusion.2, f32[512,768]{1,0:T(8,128)S(1)} %add_multiply_fusion.3), kind=kLoop, calls=%fused_computation.1 | loop fusion | flops 4718592 | bytes 12582912 | tf_op jit(solution)/shard_map/broadcast_in_dim | solution.py:111
  (35 shorter events, 2.7 us)
Async XLA Ops:
  6.5 1.2 copy-start
  6.5 54.8 %all-gather.3.cloned.1.call-start = ((), (), s32[]{:S(2)}) async-start(), calls=%async_computation | async-start | bytes 2359296 | tf_op jit(solution)/shard_map/all_gather | solution.py:92
  8.5 3.5 %copy-start.2 = (s32[1,8192]{1,0:T(1,128)S(1)}, s32[1,8192]{1,0:T(1,128)}, u32[]{:S(2)}) copy-start(s32[1,8192]{1,0:T(1,128)} %param.7) | copy-start | bytes 98308
  12.1 37.8 %copy-start.4 = (s32[6]{0:T(128)S(1)}, s32[6]{0:T(128)}, u32[]{:S(2)}) copy-start(s32[6]{0:T(128)} %param.9) | copy-start | bytes 76
  63.6 8.2 %copy-start.3 = (bf16[8192,1024]{1,0:T(8,128)(2,1)S(1)}, bf16[8192,1024]{1,0:T(8,128)(2,1)}, u32[]{:S(2)}) copy-start(bf16[8192,1024]{1,0:T(8,128)(2,1)} %shard_map.55) | copy-start | bytes 50331652
  66.3 15.9 %collective-permute-start.1 = (bf16[512,768]{1,0:T(8,128)(2,1)S(1)}, bf16[512,768]{1,0:T(8,128)(2,1)S(1)}, u32[]{:S(2)}, u32[]{:S(2)}) collective-permute-start(bf16[512,768]{1,0:T(8,128)(2,1)S(1)} %convolution_convert_fusion.6), channel_id=1, source_target_pairs={{0,8},{8,0},{16,24},{24,16},{1,9},{9,1},{17,25},{25,17},{2,10},{10... | collective-permute-start | bytes 2359304 | tf_op jit(solution)/shard_map/ppermute | solution.py:78
  69.4 18.4 %collective-permute-start = (bf16[512,768]{1,0:T(8,128)(2,1)S(1)}, bf16[512,768]{1,0:T(8,128)(2,1)S(1)}, u32[]{:S(2)}, u32[]{:S(2)}) collective-permute-start(bf16[512,768]{1,0:T(8,128)(2,1)S(1)} %convolution_convert_fusion.7), channel_id=1, source_target_pairs={{0,8},{8,0},{16,24},{24,16},{1,9},{9,1},{17,25},{25,17},{2,10},{10... | collective-permute-start | bytes 2359304 | tf_op jit(solution)/shard_map/ppermute | solution.py:78
  72.8 10.6 %collective-permute-start.4 = (bf16[512,768]{1,0:T(8,128)(2,1)S(1)}, bf16[512,768]{1,0:T(8,128)(2,1)S(1)}, u32[]{:S(2)}, u32[]{:S(2)}) collective-permute-start(bf16[512,768]{1,0:T(8,128)(2,1)S(1)} %convolution_convert_fusion.4), channel_id=1, source_target_pairs={{0,8},{8,0},{16,24},{24,16},{1,9},{9,1},{17,25},{25,17},{2,10},{10... | collective-permute-start | bytes 2359304 | tf_op jit(solution)/shard_map/ppermute | solution.py:78
  74.3 16.1 %collective-permute-start.3 = (bf16[512,768]{1,0:T(8,128)(2,1)S(1)}, bf16[512,768]{1,0:T(8,128)(2,1)S(1)}, u32[]{:S(2)}, u32[]{:S(2)}) collective-permute-start(bf16[512,768]{1,0:T(8,128)(2,1)S(1)} %convolution_convert_fusion.5), channel_id=1, source_target_pairs={{0,8},{8,0},{16,24},{24,16},{1,9},{9,1},{17,25},{25,17},{2,10},{10... | collective-permute-start | bytes 2359304 | tf_op jit(solution)/shard_map/ppermute | solution.py:78
  76.5 9.6 %collective-permute-start.7 = (bf16[512,768]{1,0:T(8,128)(2,1)S(1)}, bf16[512,768]{1,0:T(8,128)(2,1)S(1)}, u32[]{:S(2)}, u32[]{:S(2)}) collective-permute-start(bf16[512,768]{1,0:T(8,128)(2,1)S(1)} %convolution_convert_fusion.2), channel_id=1, source_target_pairs={{0,8},{8,0},{16,24},{24,16},{1,9},{9,1},{17,25},{25,17},{2,10},{10... | collective-permute-start | bytes 2359304 | tf_op jit(solution)/shard_map/ppermute | solution.py:78
  82.2 5.6 %collective-permute-start.10 = (bf16[512,768]{1,0:T(8,128)(2,1)S(1)}, bf16[512,768]{1,0:T(8,128)(2,1)S(1)}, u32[]{:S(2)}, u32[]{:S(2)}) collective-permute-start(bf16[512,768]{1,0:T(8,128)(2,1)S(1)} %convolution_convert_fusion), channel_id=1, source_target_pairs={{0,8},{8,0},{16,24},{24,16},{1,9},{9,1},{17,25},{25,17},{2,10},{10... | collective-permute-start | bytes 2359304 | tf_op jit(solution)/shard_map/ppermute | solution.py:78
  83.3 20.5 %collective-permute-start.2 = (bf16[512,768]{1,0:T(8,128)(2,1)S(1)}, bf16[512,768]{1,0:T(8,128)(2,1)S(1)}, u32[]{:S(2)}, u32[]{:S(2)}) collective-permute-start(bf16[512,768]{1,0:T(8,128)(2,1)S(1)} %add_convert_fusion.3), channel_id=1, source_target_pairs={{0,16},{8,24},{16,0},{24,8},{1,17},{9,25},{17,1},{25,9},{2,18},{10... | collective-permute-start | bytes 2359304 | tf_op jit(solution)/shard_map/ppermute | solution.py:78
  86.1 34.6 %collective-permute-start.5 = (bf16[512,768]{1,0:T(8,128)(2,1)S(1)}, bf16[512,768]{1,0:T(8,128)(2,1)S(1)}, u32[]{:S(2)}, u32[]{:S(2)}) collective-permute-start(bf16[512,768]{1,0:T(8,128)(2,1)S(1)} %add_convert_fusion.2), channel_id=1, source_target_pairs={{0,16},{8,24},{16,0},{24,8},{1,17},{9,25},{17,1},{25,9},{2,18},{10... | collective-permute-start | bytes 2359304 | tf_op jit(solution)/shard_map/ppermute | solution.py:78
  87.7 33.2 %collective-permute-start.6 = (bf16[512,768]{1,0:T(8,128)(2,1)S(1)}, bf16[512,768]{1,0:T(8,128)(2,1)S(1)}, u32[]{:S(2)}, u32[]{:S(2)}) collective-permute-start(bf16[512,768]{1,0:T(8,128)(2,1)S(1)} %convolution_convert_fusion.3), channel_id=1, source_target_pairs={{0,8},{8,0},{16,24},{24,16},{1,9},{9,1},{17,25},{25,17},{2,10},{10... | collective-permute-start | bytes 2359304 | tf_op jit(solution)/shard_map/ppermute | solution.py:78
  87.8 49.7 %collective-permute-start.8 = (bf16[512,768]{1,0:T(8,128)(2,1)S(1)}, bf16[512,768]{1,0:T(8,128)(2,1)S(1)}, u32[]{:S(2)}, u32[]{:S(2)}) collective-permute-start(bf16[512,768]{1,0:T(8,128)(2,1)S(1)} %add_convert_fusion.1), channel_id=1, source_target_pairs={{0,16},{8,24},{16,0},{24,8},{1,17},{9,25},{17,1},{25,9},{2,18},{10... | collective-permute-start | bytes 2359304 | tf_op jit(solution)/shard_map/ppermute | solution.py:78
  90.4 47.4 %collective-permute-start.9 = (bf16[512,768]{1,0:T(8,128)(2,1)S(1)}, bf16[512,768]{1,0:T(8,128)(2,1)S(1)}, u32[]{:S(2)}, u32[]{:S(2)}) collective-permute-start(bf16[512,768]{1,0:T(8,128)(2,1)S(1)} %convolution_convert_fusion.1), channel_id=1, source_target_pairs={{0,8},{8,0},{16,24},{24,16},{1,9},{9,1},{17,25},{25,17},{2,10},{10... | collective-permute-start | bytes 2359304 | tf_op jit(solution)/shard_map/ppermute | solution.py:78
  103.8 50.1 %collective-permute-start.11 = (bf16[512,768]{1,0:T(8,128)(2,1)S(1)}, bf16[512,768]{1,0:T(8,128)(2,1)S(1)}, u32[]{:S(2)}, u32[]{:S(2)}) collective-permute-start(bf16[512,768]{1,0:T(8,128)(2,1)S(1)} %add_convert_fusion), channel_id=1, source_target_pairs={{0,16},{8,24},{16,0},{24,8},{1,17},{9,25},{17,1},{25,9},{2,18},{10... | collective-permute-start | bytes 2359304 | tf_op jit(solution)/shard_map/ppermute | solution.py:78
  154.1 2.9 %copy-start.1 = (bf16[128,4096]{1,0:T(8,128)(2,1)S(1)}, bf16[128,4096]{1,0:T(8,128)(2,1)}, u32[]{:S(2)}) copy-start(bf16[128,4096]{1,0:T(8,128)(2,1)} %param.8) | copy-start | bytes 3145732
Sparse Core Ops, SparseCore 0:
  9.5 51.8 all-gather.2
